TPU v7x, 32 devices: a whole 2x2x4 slice. The times are simulated.
32 devices in a mesh: ckpt: 4 (over x, core), wide: 8 (over z, y).
Axes of the slice: x: 2, y: 2, z: 4, core: 2. Of those that a mesh axis runs over, the one named last changes fastest.
Arguments:
- codes: bfloat16 [4, 8, 8192, 1024], P('ckpt', 'wide'), may hold values from -4 to 4
- scales: float32 [4, 8, 8192, 8], P('ckpt', 'wide'), may hold values from 0.5 to 5
- example_ids: int32 [8, 8192], P('wide'), may hold values from 0 to 8191, each once within a row
- targets: bfloat16 [1024, 4096], P('wide'), may hold values from -0.09375 to 0.09375
- owners: int32 [6], replicated, may hold values from 0 to 7, as said below
Outputs:
- scores: float32 [8, 8192, 768], P('wide', 'ckpt')
Inputs may be any that keep to these rules, and one draw needn't show every extreme that they name: `example_ids`: each row is a permutation of the 8192 examples of its group. Distinct owners; owner 0 and owner 8 - 1 are always among them.
All inputs are finite; a program needn't handle non-finite values.
Results may differ from a plain program's by a relative error of at most 0.0029.
Values may be sent and summed in bfloat16 or wider, within the bound.
A program may use at most 192 MiB of HBM per device.

v0:
```python
import jax
import jax.numpy as jnp
from jax import lax
from jax.sharding import PartitionSpec as P


def from_root(shard, axis, root):
    mine = lax.axis_index(axis) == root
    return lax.psum(jnp.where(mine, shard, jnp.zeros_like(shard)), axis)


def fetch(targets, owner, width):
    piece = lax.dynamic_slice_in_dim(targets, lax.axis_index("ckpt") * width, width, 1)
    got = from_root(piece, "wide", owner)
    return lax.all_gather(got, "ckpt", axis=1, tiled=True)


def per_device(codes, scales, example_ids, targets, owners):
    width = codes.shape[-1]
    block = width // scales.shape[-1]
    feats = (codes[0, 0].astype(jnp.float32) * jnp.repeat(scales[0, 0], block, axis=-1)).astype(
        jnp.bfloat16
    )
    ordered = jnp.take(feats, example_ids[0], axis=0)
    rounds = owners.shape[0]
    contract = (((1,), (1,)), ((), ()))
    resident = lax.all_to_all(ordered, "ckpt", split_axis=0, concat_axis=1, tiled=True)
    columns = []
    for step in range(rounds):
        chosen = fetch(targets, owners[step], width)
        columns.append(
            lax.dot_general(resident, chosen, contract, preferred_element_type=jnp.float32)
        )
    result = jnp.concatenate(columns, axis=1)
    scale_factor = 1.0 / lax.axis_size("ckpt")
    return (result * scale_factor)[None]


def solution(mesh):
    return jax.shard_map(
        per_device,
        mesh=mesh,
        in_specs=(
            P("ckpt", "wide", None, None),
            P("ckpt", "wide", None, None),
            P("wide", None),
            P("wide", None),
            P(),
        ),
        out_specs=P("wide", "ckpt", None),
        check_vma=False,
    )
```

profile of v0, /device:TPU:28, one launch (start us, length us, event | category | flops | bytes accessed | tf_op | source)
XLA Modules:
  0.0 416.7 jit_solution(499906623515090295)
XLA Ops:
  6.5 3.5 copy.8
  10.1 0.8 compare_select_fusion
  10.9 10.3 %broadcast_in_dim.15 = f32[8192,8,128]{2,1,0:T(8,128)S(1)} broadcast(f32[8192,8]{1,0:T(8,128)} %copy.8), dimensions={0,1} | broadcast | bytes 33816576 | tf_op jit(solution)/shard_map/broadcast_in_dim | solution.py:21
  21.2 18.0 %fusion = bf16[8192,1024]{1,0:T(8,128)(2,1)} fusion(f32[1024,8,8,128]{3,2,1,0:T(8,128)S(1)} %bitcast.58, bf16[1,1,8192,1024]{3,2,1,0:T(8,128)(2,1)} %param.5), kind=kLoop, calls=%fused_computation.2 | loop fusion | flops 25165824 | bytes 67108864 | tf_op jit(solution)/shard_map/convert_element_type | solution.py:21
  39.1 48.4 %gather_fusion = bf16[8192,1024]{1,0:T(8,128)(2,1)} fusion(bf16[8192,1024]{1,0:T(8,128)(2,1)} %fusion, s32[8192]{0:T(1024)S(1)} %broadcast_clamp_fusion), kind=kCustom, calls=%fused_computation | custom fusion | bytes 33587200 | tf_op jit(solution)/shard_map/jit(_take)/gather | solution.py:24
  87.6 0.0 copy-start
  87.6 21.9 %copy.9 = bf16[4,2048,1024]{1,2,0:T(8,128)(2,1)} copy(bf16[4,2048,1024]{2,1,0:T(8,128)(2,1)} %bitcast.59) | data formatting | bytes 33554432 | tf_op jit(solution)/shard_map/jit(_take)/gather | solution.py:24
  109.5 0.5 broadcast.55
  110.0 0.0 copy-done
  110.0 0.7 reduce.3
  110.8 14.2 %broadcast_select_fusion = bf16[4,2048,1024]{1,2,0:T(8,128)(2,1)} fusion(bf16[4,2048,1024]{1,2,0:T(8,128)(2,1)} %copy.9, pred[4,2048]{1,0:T(4,128)(4,1)S(1)} %compare_and_fusion), kind=kLoop, calls=%fused_computation.3 | loop fusion | flops 8388608 | bytes 33562624 | tf_op jit(solution)/shard_map/jit(_take)/select_n | solution.py:24
  125.0 0.0 copy-start.1
  125.0 7.1 %all-to-all-start = ((bf16[4,2048,1024]{1,2,0:T(8,128)(2,1)}), bf16[4,2048,1024]{1,2,0:T(8,128)(2,1)}, u32[]{:S(2)}, u32[]{:S(2)}) async-start(bf16[4,2048,1024]{1,2,0:T(8,128)(2,1)} %broadcast_select_fusion), calls=%async_computation | async-start | bytes 33554432 | tf_op jit(solution)/shard_map/all_to_all | solution.py:27
  132.1 0.0 all-reduce.3.cloned.1.call-start
  132.1 0.0 copy-done.1
  132.1 0.7 fusion.7
  136.6 2.2 broadcast_select_fusion.1
  138.8 0.0 all-reduce.3.cloned.1.call-update
  138.8 0.0 all-gather.7.cloned.1.call-start
  138.8 89.4 %all-reduce.3.cloned.1.call-done = (bf16[128,1024]{1,0:T(8,128)(2,1)}, bf16[128,1024]{1,0:T(8,128)(2,1)}, bf16[128,1024]{1,0:T(8,128)(2,1)}, bf16[128,1024]{1,0:...) async-done(((bf16[128,1024]{1,0:T(8,128)(2,1)}, bf16[128,1024]{1,0:T(8,128)(2,1)}, bf16[128,1024]{1,0:T(8,128)(2,1)}, bf16[128,1024]{1,0:T(8,128)(2,1)}, ...) | async-done | bytes 1572880 | tf_op jit(solution)/shard_map/psum | solution.py:9
  228.2 0.0 all-gather.7.cloned.1.call-update
  228.3 0.0 all-gather.9.cloned.1.call-start
  228.3 0.7 all-gather.9.cloned.1.call-update
  229.0 0.0 all-gather.11.cloned.1.call-start
  229.0 0.5 all-gather.11.cloned.1.call-update
  229.6 0.0 all-gather.13.cloned.1.call-start
  229.6 0.5 all-gather.13.cloned.1.call-update
  230.2 0.0 all-gather.15.cloned.1.call-start
  230.2 0.5 all-gather.15.cloned.1.call-update
  230.7 0.2 all-gather.17.cloned.1.call-start
  231.0 0.5 all-gather.17.cloned.1.call-update
  231.5 21.7 %all-gather.7.cloned.1.call-done = bf16[128,4096]{1,0:T(8,128)(2,1)} async-done(((bf16[128,1024]{1,0:T(8,128)(2,1)}), bf16[128,4096]{1,0:T(8,128)(2,1)}) %all-gather.7.cloned.1.call-update) | async-done | bytes 1048592 | tf_op jit(solution)/shard_map/all_gather | solution.py:15
  253.2 86.4 %all-to-all-done = bf16[4,2048,1024]{1,2,0:T(8,128)(2,1)} async-done(((bf16[4,2048,1024]{1,2,0:T(8,128)(2,1)}), bf16[4,2048,1024]{1,2,0:T(8,128)(2,1)}, u32[]{:S(2)}, u32[]{:S(2)}) %all-to-all-start) | async-done | bytes 16777248 | tf_op jit(solution)/shard_map/all_to_all | solution.py:27
  339.6 9.5 %fusion.6 = f32[1,2048,768]{1,2,0:T(8,128)} fusion(bf16[128,4096]{1,0:T(8,128)(2,1)} %all-gather.7.cloned.1.call-done, bf16[2048,4096]{0,1:T(8,128)(2,1)} %bitcast.6), kind=kOutput, calls=%fused_computation.16 | convolution fusion | flops 2147483648 | bytes 18874368 | tf_op jit(solution)/shard_map/dot_general | solution.py:32
  349.0 0.0 all-gather.9.cloned.1.call-done
  349.0 9.8 %fusion.5 = f32[1,2048,768]{1,2,0:T(8,128)} fusion(f32[1,2048,768]{1,2,0:T(8,128)} %fusion.6, bf16[128,4096]{1,0:T(8,128)(2,1)} %all-gather.9.cloned.1.call-done, bf16[2048,4096]{0,1:T(8,128)(2,1)} %bitcast.6), kind=kOutput, calls=%fused_computation.14 | convolution fusion | flops 2147483648 | bytes 18874368 | tf_op jit(solution)/shard_map/dot_general | solution.py:32
  358.8 0.0 all-gather.11.cloned.1.call-done
  358.8 9.5 %fusion.4 = f32[1,2048,768]{1,2,0:T(8,128)} fusion(f32[1,2048,768]{1,2,0:T(8,128)} %fusion.5, bf16[128,4096]{1,0:T(8,128)(2,1)} %all-gather.11.cloned.1.call-done, bf16[2048,4096]{0,1:T(8,128)(2,1)} %bitcast.6), kind=kOutput, calls=%fused_computation.12 | convolution fusion | flops 2147483648 | bytes 18874368 | tf_op jit(solution)/shard_map/dot_general | solution.py:32
  368.3 0.0 all-gather.13.cloned.1.call-done
  368.3 9.4 %fusion.3 = f32[1,2048,768]{1,2,0:T(8,128)} fusion(f32[1,2048,768]{1,2,0:T(8,128)} %fusion.4, bf16[128,4096]{1,0:T(8,128)(2,1)} %all-gather.13.cloned.1.call-done, bf16[2048,4096]{0,1:T(8,128)(2,1)} %bitcast.6), kind=kOutput, calls=%fused_computation.10 | convolution fusion | flops 2147483648 | bytes 18874368 | tf_op jit(solution)/shard_map/dot_general | solution.py:32
  377.7 0.0 all-gather.15.cloned.1.call-done
  377.7 9.4 %fusion.2 = f32[1,2048,768]{1,2,0:T(8,128)} fusion(f32[1,2048,768]{1,2,0:T(8,128)} %fusion.3, bf16[128,4096]{1,0:T(8,128)(2,1)} %all-gather.15.cloned.1.call-done, bf16[2048,4096]{0,1:T(8,128)(2,1)} %bitcast.6), kind=kOutput, calls=%fused_computation.8 | convolution fusion | flops 2147483648 | bytes 18874368 | tf_op jit(solution)/shard_map/dot_general | solution.py:32
  387.1 0.0 all-gather.17.cloned.1.call-done
  387.1 9.7 %fusion.1 = f32[1,2048,768]{1,2,0:T(8,128)} fusion(f32[1,2048,768]{1,2,0:T(8,128)} %fusion.2, bf16[128,4096]{1,0:T(8,128)(2,1)} %all-gather.17.cloned.1.call-done, bf16[2048,4096]{0,1:T(8,128)(2,1)} %bitcast.6), kind=kOutput, calls=%fused_computation.6 | convolution fusion | flops 2147483648 | bytes 18874368 | tf_op jit(solution)/shard_map/dot_general | solution.py:32
  396.8 6.6 %broadcast_multiply_fusion = f32[1,2048,768]{1,2,0:T(8,128)} fusion(f32[1,2048,768]{1,2,0:T(8,128)} %fusion.1), kind=kLoop, calls=%fused_computation.4 | loop fusion | flops 1572864 | bytes 12582912 | tf_op jit(solution)/shard_map/mul | solution.py:36
  403.3 6.6 %copy.10 = f32[1,2048,768]{2,1,0:T(8,128)} copy(f32[1,2048,768]{1,2,0:T(8,128)} %broadcast_multiply_fusion) | data formatting | bytes 12582912 | tf_op jit(solution)/shard_map/mul | solution.py:36
  (3 shorter events, 0.0 us)
Async XLA Ops:
  87.6 22.4 %copy-start = (s32[1,8192]{1,0:T(1,128)S(1)}, s32[1,8192]{1,0:T(1,128)}, u32[]{:S(2)}) copy-start(s32[1,8192]{1,0:T(1,128)} %param.7) | copy-start | bytes 98308
  125.0 7.2 %copy-start.1 = (s32[6]{0:T(128)S(1)}, s32[6]{0:T(128)}, u32[]{:S(2)}) copy-start(s32[6]{0:T(128)} %param.9) | copy-start | bytes 76
  125.0 214.6 %all-to-all-start = ((bf16[4,2048,1024]{1,2,0:T(8,128)(2,1)}), bf16[4,2048,1024]{1,2,0:T(8,128)(2,1)}, u32[]{:S(2)}, u32[]{:S(2)}) async-start(bf16[4,2048,1024]{1,2,0:T(8,128)(2,1)} %broadcast_select_fusion), calls=%async_computation | async-start | bytes 33554432 | tf_op jit(solution)/shard_map/all_to_all | solution.py:27
  132.1 96.2 %all-reduce.3.cloned.1.call-start = ((), (), s32[]{:S(2)}) async-start(), calls=%async_computation.7 | async-start | bytes 3145728 | tf_op jit(solution)/shard_map/psum | solution.py:9
  138.8 114.4 %all-gather.7.cloned.1.call-start = ((), (), s32[]{:S(2)}) async-start(), calls=%async_computation.1 | async-start | bytes 1310720 | tf_op jit(solution)/shard_map/all_gather | solution.py:15
  228.3 120.8 %all-gather.9.cloned.1.call-start = ((), (), s32[]{:S(2)}) async-start(), calls=%async_computation.2 | async-start | bytes 1310720 | tf_op jit(solution)/shard_map/all_gather | solution.py:15
  229.0 129.8 %all-gather.11.cloned.1.call-start = ((), (), s32[]{:S(2)}) async-start(), calls=%async_computation.3 | async-start | bytes 1310720 | tf_op jit(solution)/shard_map/all_gather | solution.py:15
  229.6 138.7 %all-gather.13.cloned.1.call-start = ((), (), s32[]{:S(2)}) async-start(), calls=%async_computation.4 | async-start | bytes 1310720 | tf_op jit(solution)/shard_map/all_gather | solution.py:15
  230.2 147.5 %all-gather.15.cloned.1.call-start = ((), (), s32[]{:S(2)}) async-start(), calls=%async_computation.5 | async-start | bytes 1310720 | tf_op jit(solution)/shard_map/all_gather | solution.py:15
  230.7 156.4 %all-gather.17.cloned.1.call-start = ((), (), s32[]{:S(2)}) async-start(), calls=%async_computation.6 | async-start | bytes 1310720 | tf_op jit(solution)/shard_map/all_gather | solution.py:15
Sparse Core Ops, SparseCore 0:
  138.9 89.2 all-reduce.2
  229.8 23.3 all-gather.6
  254.8 22.4 all-gather.8
  278.6 22.4 all-gather.10
  302.5 22.3 all-gather.12
  326.3 18.1 all-gather.14
  346.1 16.6 all-gather.16
where the time goes:
time: 418 us; the launch traced here: 417 us
  waiting for transfers between devices  200 us (48%)
  local copies, waits for them, and re-layouts  91.9 us (22%)
  matrix products  57.2 us (14%)
  other arithmetic  42.4 us (10%)
  between operations  17.3 us (4%)
  starting transfers between devices  7.55 us (2%)
    psum x1, waiting for transfers between devices, from_root(): return lax.psum(jnp.where(mine, shard, jnp.zeros_like(shard)), axis)  89.4 us
    all_to_all x1, waiting for transfers between devices, per_device(): lax.all_to_all(ordered, 'ckpt', split_axis=0, concat_axis=1, tiled=True)  86.4 us
    gather x2, local copies, waits for them, and re-layouts, per_device(): ordered = jnp.take(feats, example_ids[0], axis=0)  70.4 us
    dot_general x6, matrix products, per_device(): lax.dot_general(resident, chosen, contract, preferred_element_type=jnp.fl...  57.2 us
    all_gather x6, waiting for transfers between devices, fetch(): return lax.all_gather(got, 'ckpt', axis=1, tiled=True)  21.7 us
    convert_element_type x1, other arithmetic, per_device(): (codes[0, 0].astype(jnp.float32) * jnp.repeat(scales[0, 0], block, axis=-...  18 us
    select_n x2, other arithmetic, per_device(): ordered = jnp.take(feats, example_ids[0], axis=0)  15 us
    broadcast_in_dim x1, local copies, waits for them, and re-layouts, per_device(): jnp.repeat(scales[0, 0], block, axis=-1)  10.3 us
  transfers between devices with their start and end apart: 8, of which 3 were waited for; matrix products, arithmetic and copies ran while one was open for 12% of the time, Pallas kernels for 0%

commit v1 on v0

--- a/solution.py
+++ b/solution.py
@@ -12,7 +12,14 @@
 def fetch(targets, owner, width):
     piece = lax.dynamic_slice_in_dim(targets, lax.axis_index("ckpt") * width, width, 1)
     got = from_root(piece, "wide", owner)
-    return lax.all_gather(got, "ckpt", axis=1, tiled=True)
+
+    def advance_slabs_on_mesh(vec, join_dim):
+        arr_now = lax.axis_size("ckpt")
+        heard = jnp.stack([vec] * arr_now)
+        base_arr = lax.all_to_all(heard, "ckpt", split_axis=0, concat_axis=0)
+        return jnp.concatenate(base_arr, axis=join_dim)
+
+    return advance_slabs_on_mesh(got, 1)
 
 
 def per_device(codes, scales, example_ids, targets, owners):

time: 418 us -> 450 us (1.077)
  blocking collectives: 0 us -> 194 us
  waiting for transfers between devices: 200 us -> 16.2 us
  matrix products: 57.2 us -> 74.2 us
  starting transfers between devices: 7.55 us -> 21.5 us
  local copies, waits for them, and re-layouts: 91.9 us -> 78.8 us
    all_to_all x0 -> x1, blocking collectives: none -> 194 us  [per_device(): lax.all_to_all(ordered, 'ckpt', split_axis=0, concat_axis=1, tiled=True)]
    psum x1, waiting for transfers between devices: 89.4 us -> 6.28 us  [from_root(): return lax.psum(jnp.where(mine, shard, jnp.zeros_like(shard)), axis)]
    all_to_all x1 -> x6, waiting for transfers between devices: 86.4 us -> 9.91 us  [advance_slabs_on_mesh(): base_arr = lax.all_to_all(heard, 'ckpt', split_axis=0, concat_axis=0)]
    gather x2 -> x1, local copies, waits for them, and re-layouts: 70.4 us -> 48.6 us  [per_device(): ordered = jnp.take(feats, example_ids[0], axis=0)]
    all_gather x6 -> x0, waiting for transfers between devices: 21.7 us -> none  [fetch(): return lax.all_gather(got, 'ckpt', axis=1, tiled=True)]
    dot_general x6, matrix products: 57.2 us -> 74.2 us  [per_device(): lax.dot_general(resident, chosen, contract, preferred_element_type=jnp.fl...]
    all_to_all x1 -> x6, starting transfers between devices: 7.1 us -> 21.5 us  [advance_slabs_on_mesh(): base_arr = lax.all_to_all(heard, 'ckpt', split_axis=0, concat_axis=0)]
    another operation x0 -> x6, local copies, waits for them, and re-layouts: none -> 7.59 us  [advance_slabs_on_mesh(): heard = jnp.stack([vec] * arr_now)]
  transfers between devices with their start and end apart: 8 -> 7, of which waited for: 3 -> 7; matrix products, arithmetic and copies ran while one was open for 12% -> 36% of each run, Pallas kernels for 0% -> 0%
where the time goes in v1:
time: 450 us; the launch traced here: 445 us
  blocking collectives  194 us (43%)
  local copies, waits for them, and re-layouts  78.8 us (18%)
  matrix products  74.2 us (16%)
  other arithmetic  42.6 us (9%)
  starting transfers between devices  21.5 us (5%)
  between operations  17.3 us (4%)
  waiting for transfers between devices  16.2 us (4%)
    all_to_all x1, blocking collectives, per_device(): lax.all_to_all(ordered, 'ckpt', split_axis=0, concat_axis=1, tiled=True)  194 us
    dot_general x6, matrix products, per_device(): lax.dot_general(resident, chosen, contract, preferred_element_type=jnp.fl...  74.2 us
    gather x1, local copies, waits for them, and re-layouts, per_device(): ordered = jnp.take(feats, example_ids[0], axis=0)  48.6 us
    all_to_all x6, starting transfers between devices, advance_slabs_on_mesh(): base_arr = lax.all_to_all(heard, 'ckpt', split_axis=0, concat_axis=0)  21.5 us
    convert_element_type x1, other arithmetic, per_device(): (codes[0, 0].astype(jnp.float32) * jnp.repeat(scales[0, 0], block, axis=-...  18 us
    select_n x2, other arithmetic, per_device(): ordered = jnp.take(feats, example_ids[0], axis=0)  14.3 us
    broadcast_in_dim x1, local copies, waits for them, and re-layouts, per_device(): jnp.repeat(scales[0, 0], block, axis=-1)  10.3 us
    all_to_all x6, waiting for transfers between devices, advance_slabs_on_mesh(): base_arr = lax.all_to_all(heard, 'ckpt', split_axis=0, concat_axis=0)  9.91 us
  transfers between devices with their start and end apart: 7, of which 7 were waited for; matrix products, arithmetic and copies ran while one was open for 36% of the time, Pallas kernels for 0%

profile of v1, /device:TPU:28, one launch (start us, length us, event | category | flops | bytes accessed | tf_op | source)
XLA Modules:
  0.0 444.6 jit_solution(7888055737200694805)
XLA Ops:
  6.5 0.0 all-reduce.3.cloned.1.call-start
  6.5 1.5 fusion.55
  11.9 2.2 broadcast_select_fusion.1
  14.1 0.0 all-reduce.3.cloned.1.call-update
  14.1 3.5 copy.8
  17.6 0.6 broadcast.67
  18.2 1.5 reduce.3
  19.8 10.3 %broadcast_in_dim.15 = f32[8192,8,128]{2,1,0:T(8,128)S(1)} broadcast(f32[8192,8]{1,0:T(8,128)} %copy.8), dimensions={0,1} | broadcast | bytes 33816576 | tf_op jit(solution)/shard_map/broadcast_in_dim | solution.py:28
  30.1 0.0 copy-start.5
  30.1 18.0 %fusion = bf16[8192,1024]{1,0:T(8,128)(2,1)} fusion(f32[1024,8,8,128]{3,2,1,0:T(8,128)S(1)} %bitcast.104, bf16[1,1,8192,1024]{3,2,1,0:T(8,128)(2,1)} %param.5), kind=kLoop, calls=%fused_computation.2 | loop fusion | flops 25165824 | bytes 67108864 | tf_op jit(solution)/shard_map/convert_element_type | solution.py:28
  48.1 0.0 copy-done.5
  48.1 48.6 %gather_fusion = bf16[8192,1024]{1,0:T(8,128)(2,1)} fusion(bf16[8192,1024]{1,0:T(8,128)(2,1)} %fusion, s32[8192]{0:T(1024)S(1)} %broadcast_clamp_fusion), kind=kCustom, calls=%fused_computation | custom fusion | bytes 33587200 | tf_op jit(solution)/shard_map/jit(_take)/gather | solution.py:31
  96.8 6.3 %all-reduce.3.cloned.1.call-done = (bf16[128,1024]{1,0:T(8,128)(2,1)}, bf16[128,1024]{1,0:T(8,128)(2,1)}, bf16[128,1024]{1,0:T(8,128)(2,1)}, bf16[128,1024]{1,0:...) async-done(((bf16[128,1024]{1,0:T(8,128)(2,1)}, bf16[128,1024]{1,0:T(8,128)(2,1)}, bf16[128,1024]{1,0:T(8,128)(2,1)}, bf16[128,1024]{1,0:T(8,128)(2,1)}, ...) | async-done | bytes 1572880 | tf_op jit(solution)/shard_map/psum | solution.py:9
  103.1 2.0 stack.12
  105.1 3.5 all-to-all-start.1
  108.7 14.2 %broadcast_select_fusion = bf16[4,2048,1024]{2,1,0:T(8,128)(2,1)} fusion(bf16[4,2048,1024]{2,1,0:T(8,128)(2,1)} %bitcast.105, pred[4,2048]{1,0:T(4,128)(4,1)S(1)} %compare_and_fusion), kind=kLoop, calls=%fused_computation.15 | loop fusion | flops 8388608 | bytes 33562624 | tf_op jit(solution)/shard_map/jit(_take)/select_n | solution.py:31
  122.9 0.0 copy-start.4
  122.9 0.2 all-to-all-done.1
  123.1 194.1 %all_to_all.43 = bf16[4,2048,1024]{2,1,0:T(8,128)(2,1)} all-to-all(bf16[4,2048,1024]{2,1,0:T(8,128)(2,1)} %broadcast_select_fusion), channel_id=1, replica_groups=mesh['ckpt'=4,'wide'=8] {'ckpt'}, dimensions={0} | all-to-all | bytes 33554432 | tf_op jit(solution)/shard_map/all_to_all | solution.py:34
  317.1 0.0 copy-start.3
  317.1 0.0 copy-done.4
  317.1 1.1 stack.13
  318.2 3.5 all-to-all-start.2
  321.8 12.4 %fusion.16 = f32[1,2048,768]{1,2,0:T(8,128)} fusion(bf16[4,2048,1024]{2,1,0:T(8,128)(2,1)} %all_to_all.43, bf16[4,128,1024]{2,1,0:T(8,128)(2,1)S(1)} %all-to-all-done.1), kind=kOutput, calls=%fused_computation.18 | convolution fusion | flops 2147483648 | bytes 18874368 | tf_op jit(solution)/shard_map/dot_general | solution.py:39
  334.1 2.0 all-to-all-done.2
  336.2 0.0 copy-done.3
  336.2 1.1 stack.14
  337.3 3.7 all-to-all-start.3
  341.0 12.4 %fusion.22 = f32[1,2048,768]{1,2,0:T(8,128)} fusion(f32[1,2048,768]{1,2,0:T(8,128)} %fusion.16, bf16[4,2048,1024]{2,1,0:T(8,128)(2,1)} %all_to_all.43, bf16[4,128,1024]{2,1,0:T(8,128)(2,1)S(1)} %all-to-all-done.2), kind=kOutput, calls=%fused_computation.20 | convolution fusion | flops 2147483648 | bytes 18874368 | tf_op jit(solution)/shard_map/dot_general | solution.py:39
  353.3 1.8 all-to-all-done.3
  355.2 0.0 copy-done.2
  355.2 1.1 stack.15
  356.3 3.5 all-to-all-start.4
  359.8 12.4 %fusion.28 = f32[1,2048,768]{1,2,0:T(8,128)} fusion(f32[1,2048,768]{1,2,0:T(8,128)} %fusion.22, bf16[4,2048,1024]{2,1,0:T(8,128)(2,1)} %all_to_all.43, bf16[4,128,1024]{2,1,0:T(8,128)(2,1)S(1)} %all-to-all-done.3), kind=kOutput, calls=%fused_computation.22 | convolution fusion | flops 2147483648 | bytes 18874368 | tf_op jit(solution)/shard_map/dot_general | solution.py:39
  372.2 2.0 all-to-all-done.4
  374.2 0.0 copy-done.1
  374.2 1.1 stack.16
  375.3 3.5 all-to-all-start.5
  378.8 12.4 %fusion.34 = f32[1,2048,768]{1,2,0:T(8,128)} fusion(f32[1,2048,768]{1,2,0:T(8,128)} %fusion.28, bf16[4,2048,1024]{2,1,0:T(8,128)(2,1)} %all_to_all.43, bf16[4,128,1024]{2,1,0:T(8,128)(2,1)S(1)} %all-to-all-done.4), kind=kOutput, calls=%fused_computation.24 | convolution fusion | flops 2147483648 | bytes 18874368 | tf_op jit(solution)/shard_map/dot_general | solution.py:39
  391.2 2.0 all-to-all-done.5
  393.2 0.0 copy-done
  393.2 1.1 stack.17
  394.4 3.7 all-to-all-start.6
  398.1 12.4 %fusion.40 = f32[1,2048,768]{1,2,0:T(8,128)} fusion(f32[1,2048,768]{1,2,0:T(8,128)} %fusion.34, bf16[4,2048,1024]{2,1,0:T(8,128)(2,1)} %all_to_all.43, bf16[4,128,1024]{2,1,0:T(8,128)(2,1)S(1)} %all-to-all-done.5), kind=kOutput, calls=%fused_computation.26 | convolution fusion | flops 2147483648 | bytes 18874368 | tf_op jit(solution)/shard_map/dot_general | solution.py:39
  410.5 1.8 all-to-all-done.6
  412.3 12.4 %fusion.46 = f32[1,2048,768]{1,2,0:T(8,128)} fusion(f32[1,2048,768]{1,2,0:T(8,128)} %fusion.40, bf16[4,2048,1024]{2,1,0:T(8,128)(2,1)} %all_to_all.43, bf16[4,128,1024]{2,1,0:T(8,128)(2,1)S(1)} %all-to-all-done.6), kind=kOutput, calls=%fused_computation.28 | convolution fusion | flops 2147483648 | bytes 18874368 | tf_op jit(solution)/shard_map/dot_general | solution.py:39
  424.6 6.6 %broadcast_multiply_fusion = f32[1,2048,768]{1,2,0:T(8,128)} fusion(f32[1,2048,768]{1,2,0:T(8,128)} %fusion.46), kind=kLoop, calls=%fused_computation.16 | loop fusion | flops 1572864 | bytes 12582912 | tf_op jit(solution)/shard_map/mul | solution.py:43
  431.2 6.6 %copy.9 = f32[1,2048,768]{2,1,0:T(8,128)} copy(f32[1,2048,768]{1,2,0:T(8,128)} %broadcast_multiply_fusion) | data formatting | bytes 12582912 | tf_op jit(solution)/shard_map/mul | solution.py:43
  (7 shorter events, 0.1 us)
Async XLA Ops:
  6.5 96.5 %all-reduce.3.cloned.1.call-start = ((), (), s32[]{:S(2)}) async-start(), calls=%async_computation.7 | async-start | bytes 3145728 | tf_op jit(solution)/shard_map/psum | solution.py:9
  30.1 18.0 %copy-start.5 = (s32[1,8192]{1,0:T(1,128)S(1)}, s32[1,8192]{1,0:T(1,128)}, u32[]{:S(2)}) copy-start(s32[1,8192]{1,0:T(1,128)} %param.7) | copy-start | bytes 98308
  105.1 17.9 %all-to-all-start.1 = ((bf16[4,128,1024]{2,1,0:T(8,128)(2,1)}), bf16[4,128,1024]{2,1,0:T(8,128)(2,1)S(1)}, u32[]{:S(2)}, u32[]{:S(2)}) async-start(bf16[4,128,1024]{2,1,0:T(8,128)(2,1)} %stack.12), calls=%async_computation.1 | async-start | bytes 2097152 | tf_op jit(solution)/shard_map/all_to_all | solution.py:19
  122.9 194.2 %copy-start.4 = (bf16[128,1024]{1,0:T(8,128)(2,1)S(1)}, bf16[128,1024]{1,0:T(8,128)(2,1)}, u32[]{:S(2)}) copy-start(bf16[128,1024]{1,0:T(8,128)(2,1)} %get-tuple-element.6) | copy-start | bytes 786436
  317.1 19.0 %copy-start.3 = (bf16[128,1024]{1,0:T(8,128)(2,1)S(1)}, bf16[128,1024]{1,0:T(8,128)(2,1)}, u32[]{:S(2)}) copy-start(bf16[128,1024]{1,0:T(8,128)(2,1)} %get-tuple-element.7) | copy-start | bytes 786436
  318.2 17.9 %all-to-all-start.2 = ((bf16[4,128,1024]{2,1,0:T(8,128)(2,1)}), bf16[4,128,1024]{2,1,0:T(8,128)(2,1)S(1)}, u32[]{:S(2)}, u32[]{:S(2)}) async-start(bf16[4,128,1024]{2,1,0:T(8,128)(2,1)} %stack.13), calls=%async_computation.2 | async-start | bytes 2097152 | tf_op jit(solution)/shard_map/all_to_all | solution.py:19
  334.1 21.1 %copy-start.2 = (bf16[128,1024]{1,0:T(8,128)(2,1)S(1)}, bf16[128,1024]{1,0:T(8,128)(2,1)}, u32[]{:S(2)}) copy-start(bf16[128,1024]{1,0:T(8,128)(2,1)} %get-tuple-element.8) | copy-start | bytes 786436
  337.3 17.9 %all-to-all-start.3 = ((bf16[4,128,1024]{2,1,0:T(8,128)(2,1)}), bf16[4,128,1024]{2,1,0:T(8,128)(2,1)S(1)}, u32[]{:S(2)}, u32[]{:S(2)}) async-start(bf16[4,128,1024]{2,1,0:T(8,128)(2,1)} %stack.14), calls=%async_computation.3 | async-start | bytes 2097152 | tf_op jit(solution)/shard_map/all_to_all | solution.py:19
  353.3 20.9 %copy-start.1 = (bf16[128,1024]{1,0:T(8,128)(2,1)S(1)}, bf16[128,1024]{1,0:T(8,128)(2,1)}, u32[]{:S(2)}) copy-start(bf16[128,1024]{1,0:T(8,128)(2,1)} %get-tuple-element.9) | copy-start | bytes 786436
  356.3 17.9 %all-to-all-start.4 = ((bf16[4,128,1024]{2,1,0:T(8,128)(2,1)}), bf16[4,128,1024]{2,1,0:T(8,128)(2,1)S(1)}, u32[]{:S(2)}, u32[]{:S(2)}) async-start(bf16[4,128,1024]{2,1,0:T(8,128)(2,1)} %stack.15), calls=%async_computation.4 | async-start | bytes 2097152 | tf_op jit(solution)/shard_map/all_to_all | solution.py:19
  372.2 21.1 %copy-start = (bf16[128,1024]{1,0:T(8,128)(2,1)S(1)}, bf16[128,1024]{1,0:T(8,128)(2,1)}, u32[]{:S(2)}) copy-start(bf16[128,1024]{1,0:T(8,128)(2,1)} %get-tuple-element.10) | copy-start | bytes 786436
  375.3 17.9 %all-to-all-start.5 = ((bf16[4,128,1024]{2,1,0:T(8,128)(2,1)}), bf16[4,128,1024]{2,1,0:T(8,128)(2,1)S(1)}, u32[]{:S(2)}, u32[]{:S(2)}) async-start(bf16[4,128,1024]{2,1,0:T(8,128)(2,1)} %stack.16), calls=%async_computation.5 | async-start | bytes 2097152 | tf_op jit(solution)/shard_map/all_to_all | solution.py:19
  394.4 17.9 %all-to-all-start.6 = ((bf16[4,128,1024]{2,1,0:T(8,128)(2,1)}), bf16[4,128,1024]{2,1,0:T(8,128)(2,1)S(1)}, u32[]{:S(2)}, u32[]{:S(2)}) async-start(bf16[4,128,1024]{2,1,0:T(8,128)(2,1)} %stack.17), calls=%async_computation.6 | async-start | bytes 2097152 | tf_op jit(solution)/shard_map/all_to_all | solution.py:19
Sparse Core Ops, SparseCore 0:
  14.2 88.8 all-reduce.2
